TPU v7x, 512 devices: a whole 4x4x16 slice. The times are simulated.
512 devices in a mesh: dp: 64 (over z, x_lo, core), seq: 8 (over x_hi, y).
Axes of the slice: x: 4 (x_hi: 2, x_lo: 2; x = x_hi * 2 + x_lo), y: 4, z: 16, core: 2. Of those that a mesh axis runs over, the one named last changes fastest.
Arguments:
- queries: bfloat16 [65536, 3072], P(('dp', 'seq')), may hold values from -6 to 6
- key_states: bfloat16 [65536, 3072], P(('dp', 'seq')), may hold values from -6 to 6
- value_states: bfloat16 [65536, 3072], P(('dp', 'seq')), may hold values from -6 to 6
- grad_out: bfloat16 [65536, 2560], P(('dp', 'seq')), may hold values from -24 to 24
- out_weight: bfloat16 [3072, 2560], P('seq', 'dp'), may hold values from -0.109375 to 0.109375
- key_blocks: int32 [24, 16, 16], replicated, may hold values from 0 to 15, as said below
- key_count: int32 [24, 16], replicated, may hold values from 5 to 16
Outputs:
- grad_queries: bfloat16 [65536, 3072], P(('dp', 'seq'))
- grad_keys: bfloat16 [65536, 3072], P(('dp', 'seq'))
- grad_weight: float32 [3072, 2560], P('seq', 'dp')
Inputs may be any that keep to these rules, and one draw needn't show every extreme that they name: The first key_count[h, b] entries of key_blocks[h, b] name distinct key blocks; later entries name the other blocks and are not used. Query blocks 0 and 15 attend all 16 blocks; every other query block attends at most 8 blocks, and some reach 8 for every head.
All inputs are finite; a program needn't handle non-finite values.
Results may differ from a plain program's by a relative error of at most 0.0079.
Values may be sent and summed in bfloat16 or wider, within the bound.
A program may use at most 64 MiB of HBM per device.

v0:
```python
import jax
import jax.numpy as jnp
from jax import lax
from jax.sharding import PartitionSpec as P

HEADS = 24
HD = 128
BLK = 64
RANDB = 3


def forward_rows(query_rows, key_rows, value_rows, live_keys):
    scores = jnp.einsum(
        "rqd,rkd->rqk", query_rows, key_rows, preferred_element_type=jnp.float32
    ) * HD ** (-0.5)
    if live_keys is not None:
        scores = jnp.where(live_keys[:, None, :], scores, -jnp.inf)
    row_max = jnp.max(scores, axis=-1, keepdims=True)
    expo = jnp.exp(scores - row_max)
    probs = expo / jnp.sum(expo, axis=-1, keepdims=True)
    head_out = jnp.einsum(
        "rqk,rkd->rqd", probs.astype(jnp.bfloat16), value_rows, preferred_element_type=jnp.float32
    )
    return (probs, head_out.astype(jnp.bfloat16))


def backward_rows(query_rows, key_rows, value_rows, grad_rows, probs):
    dprob = jnp.einsum("rqd,rkd->rqk", grad_rows, value_rows, preferred_element_type=jnp.float32)
    row_delta = jnp.sum(probs * dprob, axis=-1, keepdims=True)
    dscore = (probs * (dprob - row_delta) * HD ** (-0.5)).astype(jnp.bfloat16)
    grad_q = jnp.einsum("rqk,rkd->rqd", dscore, key_rows, preferred_element_type=jnp.float32)
    grad_k = jnp.einsum("rqk,rqd->rkd", dscore, query_rows, preferred_element_type=jnp.float32)
    return (grad_q, grad_k)


def arrange(head_item):
    query_head, key_head, value_head, grad_head, block_list, block_count = head_item
    seq_length = query_head.shape[0]
    block_total = seq_length // BLK
    slot_count = min(block_total, 5 + RANDB)
    middle = block_total - 2
    query_blocks = query_head.reshape(block_total, BLK, HD)
    key_blocks_here = key_head.reshape(block_total, BLK, HD)
    value_blocks = value_head.reshape(block_total, BLK, HD)
    grad_blocks = grad_head.reshape(block_total, BLK, HD)
    chosen = block_list[1 : block_total - 1, :slot_count]
    live_keys = jnp.repeat(
        jnp.arange(slot_count)[None, :] < block_count[1 : block_total - 1, None], BLK, axis=1
    )
    mid_keys = key_blocks_here[chosen].reshape(middle, slot_count * BLK, HD)
    mid_values = value_blocks[chosen].reshape(middle, slot_count * BLK, HD)
    middle_group = (
        query_blocks[1 : block_total - 1],
        mid_keys,
        mid_values,
        grad_blocks[1 : block_total - 1],
        live_keys,
    )
    edge_queries = jnp.stack((query_blocks[0], query_blocks[block_total - 1]))
    edge_grads = jnp.stack((grad_blocks[0], grad_blocks[block_total - 1]))
    edge_keys = jnp.broadcast_to(key_head[None], (2, seq_length, HD))
    edge_values = jnp.broadcast_to(value_head[None], (2, seq_length, HD))
    edge_group = (edge_queries, edge_keys, edge_values, edge_grads, None)
    return (middle_group, edge_group, chosen)


def join_rows(edge_part, middle_part):
    return jnp.concatenate((edge_part[:1], middle_part, edge_part[1:]), axis=0).reshape(-1, HD)


def attend_full(head_item):
    middle_group, edge_group, chosen = arrange(head_item)
    mid_probs, mid_out = forward_rows(
        middle_group[0], middle_group[1], middle_group[2], middle_group[4]
    )
    edge_probs, edge_out = forward_rows(edge_group[0], edge_group[1], edge_group[2], None)
    mid_dq, mid_dk = backward_rows(
        middle_group[0], middle_group[1], middle_group[2], middle_group[3], mid_probs
    )
    edge_dq, edge_dk = backward_rows(
        edge_group[0], edge_group[1], edge_group[2], edge_group[3], edge_probs
    )
    block_total = head_item[0].shape[0] // BLK
    slot_count = chosen.shape[1]
    spread = (chosen[:, :, None] == jnp.arange(block_total)[None, None, :]).astype(jnp.float32)
    key_sum = jnp.einsum(
        "msn,msbd->nbd",
        spread,
        mid_dk.reshape(chosen.shape[0], slot_count, BLK, HD),
        precision=lax.Precision.HIGHEST,
    ).reshape(-1, HD)
    key_sum = key_sum + jnp.sum(edge_dk, axis=0)
    grad_query = join_rows(edge_dq, mid_dq).astype(jnp.bfloat16)
    return (join_rows(edge_out, mid_out), grad_query, key_sum.astype(jnp.bfloat16))


def project_back(whole_grad, out_weight):
    whole_rows = lax.all_gather(out_weight, "dp", axis=1, tiled=True)
    return lax.dot_general(
        whole_grad, whole_rows, (((1,), (1,)), ((), ())), preferred_element_type=jnp.float32
    )


def reduce_grads(head_outputs, whole_grad):
    local_count = head_outputs.shape[0]
    local_sum = jnp.einsum(
        "hld,lc->hdc", head_outputs, whole_grad, preferred_element_type=jnp.float32
    )
    local_sum = local_sum.reshape(local_count * HD, whole_grad.shape[1])
    return lax.psum_scatter(local_sum, "dp", scatter_dimension=1, tiled=True)


def per_device(queries, key_states, value_states, grad_out, out_weight, key_blocks, key_count):
    group_size = lax.axis_size("seq")
    local_heads = HEADS // group_size
    query_all, key_all, value_all = (
        lax.all_to_all(queries, "seq", split_axis=1, concat_axis=0, tiled=True),
        lax.all_to_all(key_states, "seq", split_axis=1, concat_axis=0, tiled=True),
        lax.all_to_all(value_states, "seq", split_axis=1, concat_axis=0, tiled=True),
    )
    whole_grad = lax.all_gather(grad_out, "seq", axis=0, tiled=True)
    seq_length = query_all.shape[0]
    first_head = lax.axis_index("seq") * local_heads
    lists_here = lax.dynamic_slice_in_dim(key_blocks, first_head, local_heads, 0)
    counts_here = lax.dynamic_slice_in_dim(key_count, first_head, local_heads, 0)
    grad_heads = project_back(whole_grad, out_weight).astype(jnp.bfloat16)

    def split_heads(array_in):
        return array_in.reshape(seq_length, local_heads, HD).transpose(1, 0, 2)

    def merge_heads(array_in):
        return array_in.transpose(1, 0, 2).reshape(seq_length, local_heads * HD)

    stacked = (
        split_heads(query_all),
        split_heads(key_all),
        split_heads(value_all),
        split_heads(grad_heads),
        lists_here,
        counts_here,
    )
    head_outputs, grad_q, grad_k = lax.map(attend_full, stacked)
    weight_part = reduce_grads(head_outputs, whole_grad)
    grad_queries, grad_keys = (
        lax.all_to_all(merge_heads(grad_q), "seq", split_axis=0, concat_axis=1, tiled=True),
        lax.all_to_all(merge_heads(grad_k), "seq", split_axis=0, concat_axis=1, tiled=True),
    )
    return (grad_queries, grad_keys, weight_part)


def solution(mesh):
    return jax.shard_map(
        per_device,
        mesh=mesh,
        in_specs=(
            P(("dp", "seq"), None),
            P(("dp", "seq"), None),
            P(("dp", "seq"), None),
            P(("dp", "seq"), None),
            P("seq", "dp"),
            P(),
            P(),
        ),
        out_specs=(P(("dp", "seq"), None), P(("dp", "seq"), None), P("seq", "dp")),
        check_vma=False,
    )
```

profile of v0, /device:TPU:8, one launch (start us, length us, event | category | flops | bytes accessed | tf_op | source)
XLA Modules:
  0.0 640.3 jit_solution(14986661294399659930)
XLA Ops:
  8.7 2.3 copy.56
  11.0 9.3 %all-to-all-start = ((bf16[128,8,384]{0,2,1:T(8,128)(2,1)}), bf16[128,8,384]{0,2,1:T(8,128)(2,1)S(1)}, u32[]{:S(2)}, u32[]{:S(2)}) async-start(bf16[128,8,384]{0,2,1:T(8,128)(2,1)} %bitcast.19), calls=%async_computation | async-start | bytes 1572864 | tf_op jit(solution)/shard_map/all_to_all | solution.py:117
  21.4 8.7 %all-to-all-done = bf16[128,8,384]{0,2,1:T(8,128)(2,1)S(1)} async-done(((bf16[128,8,384]{0,2,1:T(8,128)(2,1)}), bf16[128,8,384]{0,2,1:T(8,128)(2,1)S(1)}, u32[]{:S(2)}, u32[]{:S(2)}) %all-to-all-start) | async-done | bytes 786464 | tf_op jit(solution)/shard_map/all_to_all | solution.py:117
  30.1 5.4 all-to-all-start.1
  35.5 1.2 copy.60
  36.6 11.0 %all-to-all-done.1 = bf16[128,8,384]{0,2,1:T(8,128)(2,1)S(1)} async-done(((bf16[128,8,384]{0,2,1:T(8,128)(2,1)}), bf16[128,8,384]{0,2,1:T(8,128)(2,1)S(1)}, u32[]{:S(2)}, u32[]{:S(2)}) %all-to-all-start.1) | async-done | bytes 786464 | tf_op jit(solution)/shard_map/all_to_all | solution.py:118
  47.6 4.9 all-to-all-start.2
  54.9 1.3 reshape.100
  56.2 8.3 %all-to-all-done.2 = bf16[128,8,384]{0,2,1:T(8,128)(2,1)S(1)} async-done(((bf16[128,8,384]{0,2,1:T(8,128)(2,1)}), bf16[128,8,384]{0,2,1:T(8,128)(2,1)S(1)}, u32[]{:S(2)}, u32[]{:S(2)}) %all-to-all-start.2) | async-done | bytes 786464 | tf_op jit(solution)/shard_map/all_to_all | solution.py:119
  65.0 1.2 reshape.101
  66.2 70.3 %all-gather.5.cloned.1.call-done = bf16[384,2560]{0,1:T(8,128)(2,1)} async-done(((bf16[384,40]{0,1:T(8,128)(2,1)}), bf16[384,2560]{0,1:T(8,128)(2,1)}) %all-gather.5.cloned.1.call-update) | async-done | bytes 1966096 | tf_op jit(solution)/shard_map/all_gather | solution.py:98
  136.6 93.7 %all-gather.3.cloned.1.call-done = bf16[1024,2560]{1,0:T(8,128)(2,1)} async-done(((bf16[128,2560]{1,0:T(8,128)(2,1)}), bf16[1024,2560]{1,0:T(8,128)(2,1)}) %all-gather.3.cloned.1.call-update) | async-done | bytes 5242896 | tf_op jit(solution)/shard_map/all_gather | solution.py:121
  230.3 5.3 convolution_convert_fusion.3
  235.7 1.2 copy.64
  236.8 152.2 %while.14 = (s32[]{:T(128)}, bf16[3,1024,128]{2,1,0:T(8,128)(2,1)}, bf16[3,1024,128]{2,1,0:T(8,128)(2,1)}, bf16[3,1024,128]{2,1,0:T(8,128)(2,1)}, bf16[3,1024,12...) while((s32[]{:T(128)}, bf16[3,1024,128]{2,1,0:T(8,128)(2,1)}, ...), condition=%wide.region_7.8_spmd, body=%wide.region_0.7_spmd.sunk | while | flops 979120320 | bytes 70489952 | solution.py:142
  246.1 2.1 gather_fusion.1
  248.2 3.5 fusion.160
  252.5 1.8 fusion.162
  254.3 3.7 convolution_convert_fusion.9
  258.0 8.7 %fusion.163 = bf16[14,64,128]{2,1,0:T(8,128)(2,1)} fusion(bf16[14,512,128]{2,1,0:T(8,128)(2,1)S(1)} %bitcast.145, f32[14,64,512]{2,1,0:T(8,128)} %fusion.160, f32[14,64,512]{2,1,0:T(8,128)} %get-tuple-element.217, f32[14,64]{1,0:T(8,128)S(1)} %get-tuple-element.218), kind=kOutput, calls=%fused_computation.27.clone.1 | convolution fusion | flops 120767872 | bytes 5737984 | tf_op jit(solution)/shard_map/while/body/eval_jaxpr/rqk,rkd->rqd/dot_general | solution.py:31
  266.7 10.8 %fusion.165 = f32[14,512,128]{2,1,0:T(8,128)} fusion(bf16[14,64,128]{2,1,0:T(8,128)(2,1)S(1)} %bitcast.152, f32[14,64,512]{2,1,0:T(8,128)} %fusion.160, f32[14,64,512]{2,1,0:T(8,128)} %get-tuple-element.217, f32[14,64]{1,0:T(8,128)S(1)} %get-tuple-element.218), kind=kOutput, calls=%fused_computation.14.clone.1 | convolution fusion | flops 120653184 | bytes 7572992 | tf_op jit(solution)/shard_map/while/body/eval_jaxpr/rqk,rqd->rkd/dot_general | solution.py:32
  277.5 6.1 fusion.166
  283.8 2.4 fusion.167
  296.8 2.1 gather_fusion.1
  298.9 3.5 fusion.160
  303.2 1.8 fusion.162
  305.0 3.7 convolution_convert_fusion.9
  308.7 8.7 %fusion.163 = bf16[14,64,128]{2,1,0:T(8,128)(2,1)} fusion(bf16[14,512,128]{2,1,0:T(8,128)(2,1)S(1)} %bitcast.145, f32[14,64,512]{2,1,0:T(8,128)} %fusion.160, f32[14,64,512]{2,1,0:T(8,128)} %get-tuple-element.217, f32[14,64]{1,0:T(8,128)S(1)} %get-tuple-element.218), kind=kOutput, calls=%fused_computation.27.clone.1 | convolution fusion | flops 120767872 | bytes 5737984 | tf_op jit(solution)/shard_map/while/body/eval_jaxpr/rqk,rkd->rqd/dot_general | solution.py:31
  317.4 10.8 %fusion.165 = f32[14,512,128]{2,1,0:T(8,128)} fusion(bf16[14,64,128]{2,1,0:T(8,128)(2,1)S(1)} %bitcast.152, f32[14,64,512]{2,1,0:T(8,128)} %fusion.160, f32[14,64,512]{2,1,0:T(8,128)} %get-tuple-element.217, f32[14,64]{1,0:T(8,128)S(1)} %get-tuple-element.218), kind=kOutput, calls=%fused_computation.14.clone.1 | convolution fusion | flops 120653184 | bytes 7572992 | tf_op jit(solution)/shard_map/while/body/eval_jaxpr/rqk,rqd->rkd/dot_general | solution.py:32
  328.2 6.1 fusion.166
  334.5 2.5 fusion.167
  347.6 2.1 gather_fusion.1
  349.7 3.5 fusion.160
  353.9 1.8 fusion.162
  355.7 3.7 convolution_convert_fusion.9
  359.5 8.7 %fusion.163 = bf16[14,64,128]{2,1,0:T(8,128)(2,1)} fusion(bf16[14,512,128]{2,1,0:T(8,128)(2,1)S(1)} %bitcast.145, f32[14,64,512]{2,1,0:T(8,128)} %fusion.160, f32[14,64,512]{2,1,0:T(8,128)} %get-tuple-element.217, f32[14,64]{1,0:T(8,128)S(1)} %get-tuple-element.218), kind=kOutput, calls=%fused_computation.27.clone.1 | convolution fusion | flops 120767872 | bytes 5737984 | tf_op jit(solution)/shard_map/while/body/eval_jaxpr/rqk,rkd->rqd/dot_general | solution.py:31
  368.2 10.8 %fusion.165 = f32[14,512,128]{2,1,0:T(8,128)} fusion(bf16[14,64,128]{2,1,0:T(8,128)(2,1)S(1)} %bitcast.152, f32[14,64,512]{2,1,0:T(8,128)} %fusion.160, f32[14,64,512]{2,1,0:T(8,128)} %get-tuple-element.217, f32[14,64]{1,0:T(8,128)S(1)} %get-tuple-element.218), kind=kOutput, calls=%fused_computation.14.clone.1 | convolution fusion | flops 120653184 | bytes 7572992 | tf_op jit(solution)/shard_map/while/body/eval_jaxpr/rqk,rqd->rkd/dot_general | solution.py:32
  379.0 6.1 fusion.166
  385.3 2.4 fusion.167
  389.0 6.9 %fusion.81 = f32[3,128,2560]{2,1,0:T(8,128)} fusion(bf16[3,1024,128]{2,1,0:T(8,128)(2,1)} %get-tuple-element.59, bf16[1024,2560]{1,0:T(8,128)(2,1)} %all-gather.3.cloned.1.call-done), kind=kOutput, calls=%fused_computation.93 | convolution fusion | flops 2013265920 | bytes 9961472 | tf_op jit(solution)/shard_map/hld,lc->hdc/dot_general | solution.py:106
  395.9 5.6 copy.73
  404.1 5.2 all-to-all-start.4
  410.8 10.5 %all-to-all-done.4 = bf16[8,128,384]{1,2,0:T(8,128)(2,1)S(1)} async-done(((bf16[8,128,384]{1,2,0:T(8,128)(2,1)}), bf16[8,128,384]{1,2,0:T(8,128)(2,1)S(1)}, u32[]{:S(2)}, u32[]{:S(2)}) %all-to-all-start.4) | async-done | bytes 786464 | tf_op jit(solution)/shard_map/all_to_all | solution.py:146
  421.3 5.1 all-to-all-start.3
  426.3 1.2 copy.75
  427.5 12.9 %all-to-all-done.3 = bf16[8,128,384]{1,2,0:T(8,128)(2,1)S(1)} async-done(((bf16[8,128,384]{1,2,0:T(8,128)(2,1)}), bf16[8,128,384]{1,2,0:T(8,128)(2,1)S(1)}, u32[]{:S(2)}, u32[]{:S(2)}) %all-to-all-start.3) | async-done | bytes 786464 | tf_op jit(solution)/shard_map/all_to_all | solution.py:145
  440.4 1.2 copy.74
  441.5 192.2 %reduce-scatter.5.cloned.1.call-done = f32[384,40]{0,1:T(8,128)} async-done(((f32[384,2560]{0,1:T(8,128)}), f32[384,40]{0,1:T(8,128)}) %reduce-scatter.5.cloned.1.call-update) | async-done | bytes 61456
  (201 shorter events, 43.6 us)
Async XLA Ops:
  7.2 45.5 %copy-start = (s32[24,16,16]{0,2,1:T(8,128)S(1)}, s32[24,16,16]{0,2,1:T(8,128)}, u32[]{:S(2)}) copy-start(s32[24,16,16]{0,2,1:T(8,128)} %param.14) | copy-start | bytes 73732
  7.2 129.4 %all-gather.5.cloned.1.call-start = ((), (), s32[]{:S(2)}) async-start(), calls=%async_computation.7 | async-start | bytes 1996800 | tf_op jit(solution)/shard_map/all_gather | solution.py:98
  7.9 12.3 %copy-start.8 = (bf16[128,3072]{1,0:T(8,128)(2,1)S(1)}, bf16[128,3072]{1,0:T(8,128)(2,1)}, u32[]{:S(2)}) copy-start(bf16[128,3072]{1,0:T(8,128)(2,1)} %param.10) | copy-start | bytes 2359300
  7.9 222.4 %all-gather.3.cloned.1.call-start = ((), (), s32[]{:S(2)}) async-start(), calls=%async_computation.6 | async-start | bytes 5898240 | tf_op jit(solution)/shard_map/all_gather | solution.py:121
  11.0 19.1 %all-to-all-start = ((bf16[128,8,384]{0,2,1:T(8,128)(2,1)}), bf16[128,8,384]{0,2,1:T(8,128)(2,1)S(1)}, u32[]{:S(2)}, u32[]{:S(2)}) async-start(bf16[128,8,384]{0,2,1:T(8,128)(2,1)} %bitcast.19), calls=%async_computation | async-start | bytes 1572864 | tf_op jit(solution)/shard_map/all_to_all | solution.py:117
  20.2 15.2 %copy-start.9 = (bf16[128,3072]{1,0:T(8,128)(2,1)S(1)}, bf16[128,3072]{1,0:T(8,128)(2,1)}, u32[]{:S(2)}) copy-start(bf16[128,3072]{1,0:T(8,128)(2,1)} %param.11) | copy-start | bytes 2359300
  30.1 17.5 %all-to-all-start.1 = ((bf16[128,8,384]{0,2,1:T(8,128)(2,1)}), bf16[128,8,384]{0,2,1:T(8,128)(2,1)S(1)}, u32[]{:S(2)}, u32[]{:S(2)}) async-start(bf16[128,8,384]{0,2,1:T(8,128)(2,1)} %bitcast.22), calls=%async_computation.1 | async-start | bytes 1572864 | tf_op jit(solution)/shard_map/all_to_all | solution.py:118
  35.5 17.0 %copy-start.14 = (s32[24,16]{0,1:T(8,128)S(1)}, s32[24,16]{0,1:T(8,128)}, u32[]{:S(2)}) copy-start(s32[24,16]{0,1:T(8,128)} %param.15) | copy-start | bytes 4612
  47.6 16.9 %all-to-all-start.2 = ((bf16[128,8,384]{0,2,1:T(8,128)(2,1)}), bf16[128,8,384]{0,2,1:T(8,128)(2,1)S(1)}, u32[]{:S(2)}, u32[]{:S(2)}) async-start(bf16[128,8,384]{0,2,1:T(8,128)(2,1)} %bitcast.25), calls=%async_computation.2 | async-start | bytes 1572864 | tf_op jit(solution)/shard_map/all_to_all | solution.py:119
  52.5 581.3 %reduce-scatter.5.cloned.1.call-start = ((), (), s32[]{:S(2)}) async-start(), calls=%async_computation.8 | async-start | bytes 3993600
  236.8 2.1 copy-start.15
  236.9 3.6 copy-start.3
  243.1 0.9 copy-start.2
  243.6 1.0 copy-start.12
  252.5 1.8 copy-start.1
  277.5 6.3 copy-start.13
  283.6 2.7 copy-start.5
  283.8 2.5 copy-start.6
  283.8 2.5 copy-start.7
  286.3 1.3 copy-start.4
  286.3 1.3 copy-start.16
  287.6 2.1 copy-start.15
  287.6 3.6 copy-start.3
  293.8 0.9 copy-start.2
  294.3 1.0 copy-start.12
  303.2 1.8 copy-start.1
  328.2 6.3 copy-start.13
  334.3 2.7 copy-start.5
  334.5 2.6 copy-start.6
  334.5 2.6 copy-start.7
  337.0 1.3 copy-start.4
  337.0 1.3 copy-start.16
  338.3 2.1 copy-start.15
  338.3 3.6 copy-start.3
  344.5 0.9 copy-start.2
  345.0 1.0 copy-start.12
  353.9 1.8 copy-start.1
  379.0 6.3 copy-start.13
  385.1 2.7 copy-start.5
  385.2 2.5 copy-start.6
  385.3 2.5 copy-start.7
  387.7 1.3 copy-start.4
  387.7 1.3 copy-start.16
  401.5 1.1 copy-start.10
  403.1 6.2 copy-start.11
  404.1 17.2 %all-to-all-start.4 = ((bf16[8,128,384]{1,2,0:T(8,128)(2,1)}), bf16[8,128,384]{1,2,0:T(8,128)(2,1)S(1)}, u32[]{:S(2)}, u32[]{:S(2)}) async-start(bf16[8,128,384]{1,2,0:T(8,128)(2,1)} %copy.71), calls=%async_computation.4 | async-start | bytes 1572864 | tf_op jit(solution)/shard_map/all_to_all | solution.py:146
  421.3 19.1 %all-to-all-start.3 = ((bf16[8,128,384]{1,2,0:T(8,128)(2,1)}), bf16[8,128,384]{1,2,0:T(8,128)(2,1)S(1)}, u32[]{:S(2)}, u32[]{:S(2)}) async-start(bf16[8,128,384]{1,2,0:T(8,128)(2,1)} %copy.69), calls=%async_computation.3 | async-start | bytes 1572864 | tf_op jit(solution)/shard_map/all_to_all | solution.py:145
Sparse Core Ops, SparseCore 0:
  10.2 126.3 all-gather.4
  139.7 90.5 all-gather.2
  401.6 232.0 reduce-scatter.4
where the time goes:
time: 642 us; the launch traced here: 640 us
  waiting for transfers between devices  409 us (64%)
  matrix products  126 us (20%)
  local copies, waits for them, and re-layouts  55.3 us (9%)
  starting transfers between devices  29.9 us (5%)
  between operations  13.9 us (2%)
    unnamed x4, waiting for transfers between devices  194 us
    all_gather x1, waiting for transfers between devices, per_device(): whole_grad = lax.all_gather(grad_out, 'seq', axis=0, tiled=True)  93.7 us
    all_gather x1, waiting for transfers between devices, project_back(): whole_rows = lax.all_gather(out_weight, 'dp', axis=1, tiled=True)  70.3 us
    dot_general x6, matrix products, backward_rows(): jnp.einsum('rqk,rqd->rkd', dscore, query_rows, preferred_element_type=jnp...  39.7 us
    dot_general x6, matrix products, backward_rows(): jnp.einsum('rqk,rkd->rqd', dscore, key_rows, preferred_element_type=jnp.f...  27.4 us
    dot_general x3, matrix products, attend_full(): jnp.einsum('msn,msbd->nbd', spread, mid_dk.reshape(chosen.shape[0], slot_...  18.3 us
    dot_general x6, matrix products, forward_rows(): jnp.einsum('rqk,rkd->rqd', probs.astype(jnp.bfloat16), value_rows, prefer...  12.9 us
    all_to_all x1, waiting for transfers between devices, per_device(): lax.all_to_all(merge_heads(grad_q), 'seq', split_axis=0, concat_axis=1, t...  12.9 us
  transfers between devices with their start and end apart: 8, of which 8 were waited for; matrix products, arithmetic and copies ran while one was open for 2% of the time, Pallas kernels for 0%

commit v1 on v0

--- a/solution.py
+++ b/solution.py
@@ -95,7 +95,10 @@
 
 
 def project_back(whole_grad, out_weight):
-    whole_rows = lax.all_gather(out_weight, "dp", axis=1, tiled=True)
+    size = lax.axis_size("dp")
+    blocks = jnp.stack([out_weight for _ in range(size)])
+    blocks = lax.all_to_all(blocks, "dp", split_axis=0, concat_axis=0)
+    whole_rows = jnp.concatenate(blocks, axis=1)
     return lax.dot_general(
         whole_grad, whole_rows, (((1,), (1,)), ((), ())), preferred_element_type=jnp.float32
     )

time: 642 us -> 584 us (0.910)
  waiting for transfers between devices: 409 us -> 315 us
  blocking collectives: 0 us -> 20.6 us
  starting transfers between devices: 29.9 us -> 43.9 us
    all_gather x1, waiting for transfers between devices: 93.7 us -> 0.01 us  [per_device(): whole_grad = lax.all_gather(grad_out, 'seq', axis=0, tiled=True)]
    all_to_all x1, waiting for transfers between devices: 8.29 us -> 89.8 us  [project_back(): blocks = lax.all_to_all(blocks, 'dp', split_axis=0, concat_axis=0)]
    all_gather x1 -> x0, waiting for transfers between devices: 70.3 us -> none  [project_back(): whole_rows = lax.all_gather(out_weight, 'dp', axis=1, tiled=True)]
    all_to_all x0 -> x1, blocking collectives: none -> 20.6 us  [per_device(): lax.all_to_all(value_states, 'seq', split_axis=1, concat_axis=0, tiled=True)]
    all_to_all x1, starting transfers between devices: 4.9 us -> 18.9 us  [project_back(): blocks = lax.all_to_all(blocks, 'dp', split_axis=0, concat_axis=0)]
    unnamed x4 -> x3, waiting for transfers between devices: 194 us -> 187 us
  transfers between devices with their start and end apart: 8 -> 7, of which waited for: 8 -> 6; matrix products, arithmetic and copies ran while one was open for 2% -> 2% of each run, Pallas kernels for 0% -> 0%
where the time goes in v1:
time: 584 us; the launch traced here: 582 us
  waiting for transfers between devices  315 us (54%)
  matrix products  126 us (22%)
  local copies, waits for them, and re-layouts  56 us (10%)
  starting transfers between devices  43.9 us (8%)
  blocking collectives  20.6 us (4%)
  between operations  14.2 us (2%)
  other arithmetic  5.88 us (1%)
    unnamed x3, waiting for transfers between devices  187 us
    all_to_all x1, waiting for transfers between devices, project_back(): blocks = lax.all_to_all(blocks, 'dp', split_axis=0, concat_axis=0)  89.8 us
    dot_general x6, matrix products, backward_rows(): jnp.einsum('rqk,rqd->rkd', dscore, query_rows, preferred_element_type=jnp...  39.7 us
    dot_general x6, matrix products, backward_rows(): jnp.einsum('rqk,rkd->rqd', dscore, key_rows, preferred_element_type=jnp.f...  27.4 us
    all_to_all x1, blocking collectives, per_device(): lax.all_to_all(value_states, 'seq', split_axis=1, concat_axis=0, tiled=True)  20.6 us
    all_to_all x1, starting transfers between devices, project_back(): blocks = lax.all_to_all(blocks, 'dp', split_axis=0, concat_axis=0)  18.9 us
    dot_general x3, matrix products, attend_full(): jnp.einsum('msn,msbd->nbd', spread, mid_dk.reshape(chosen.shape[0], slot_...  18.3 us
    dot_general x6, matrix products, forward_rows(): jnp.einsum('rqk,rkd->rqd', probs.astype(jnp.bfloat16), value_rows, prefer...  12.9 us
  transfers between devices with their start and end apart: 7, of which 6 were waited for; matrix products, arithmetic and copies ran while one was open for 2% of the time, Pallas kernels for 0%

profile of v1, /device:TPU:8, one launch (start us, length us, event | category | flops | bytes accessed | tf_op | source)
XLA Modules:
  0.0 582.1 jit_solution(14631367050300641687)
XLA Ops:
  7.2 2.4 copy.57
  9.6 9.3 %all-to-all-start = ((bf16[128,8,384]{0,2,1:T(8,128)(2,1)}), bf16[128,8,384]{0,2,1:T(8,128)(2,1)S(1)}, u32[]{:S(2)}, u32[]{:S(2)}) async-start(bf16[128,8,384]{0,2,1:T(8,128)(2,1)} %bitcast.19), calls=%async_computation | async-start | bytes 1572864 | tf_op jit(solution)/shard_map/all_to_all | solution.py:120
  19.6 1.2 copy.59
  20.7 7.9 %all-to-all-done = bf16[128,8,384]{0,2,1:T(8,128)(2,1)S(1)} async-done(((bf16[128,8,384]{0,2,1:T(8,128)(2,1)}), bf16[128,8,384]{0,2,1:T(8,128)(2,1)S(1)}, u32[]{:S(2)}, u32[]{:S(2)}) %all-to-all-start) | async-done | bytes 786464 | tf_op jit(solution)/shard_map/all_to_all | solution.py:120
  28.7 5.4 all-to-all-start.1
  34.4 10.7 %all-to-all-done.1 = bf16[128,8,384]{0,2,1:T(8,128)(2,1)S(1)} async-done(((bf16[128,8,384]{0,2,1:T(8,128)(2,1)}), bf16[128,8,384]{0,2,1:T(8,128)(2,1)S(1)}, u32[]{:S(2)}, u32[]{:S(2)}) %all-to-all-start.1) | async-done | bytes 786464 | tf_op jit(solution)/shard_map/all_to_all | solution.py:121
  45.2 20.6 %all_to_all.91 = bf16[128,8,384]{0,2,1:T(8,128)(2,1)S(1)} all-to-all(bf16[128,8,384]{0,2,1:T(8,128)(2,1)S(1)} %bitcast.165), channel_id=1, replica_groups=mesh['dp'=64,'seq'=8] {'seq'}, dimensions={1} | all-to-all | bytes 1572864 | tf_op jit(solution)/shard_map/all_to_all | solution.py:122
  65.8 1.5 stack.6
  67.3 18.9 %all-to-all-start.3 = ((bf16[64,384,40]{1,2,0:T(8,128)(2,1)}), bf16[64,384,40]{1,2,0:T(8,128)(2,1)}, u32[]{:S(2)}, u32[]{:S(2)}) async-start(bf16[64,384,40]{1,2,0:T(8,128)(2,1)} %stack.6), calls=%async_computation.3 | async-start | bytes 3932160 | tf_op jit(solution)/shard_map/all_to_all | solution.py:100
  88.8 1.3 reshape.108
  90.6 1.2 reshape.109
  91.8 89.8 %all-to-all-done.3 = bf16[64,384,40]{1,2,0:T(8,128)(2,1)} async-done(((bf16[64,384,40]{1,2,0:T(8,128)(2,1)}), bf16[64,384,40]{1,2,0:T(8,128)(2,1)}, u32[]{:S(2)}, u32[]{:S(2)}) %all-to-all-start.3) | async-done | bytes 1966112 | tf_op jit(solution)/shard_map/all_to_all | solution.py:100
  181.6 5.3 convolution_convert_fusion.3
  187.0 1.2 copy.65
  188.2 152.2 %while.14 = (s32[]{:T(128)}, bf16[3,1024,128]{2,1,0:T(8,128)(2,1)}, bf16[3,1024,128]{2,1,0:T(8,128)(2,1)}, bf16[3,1024,128]{2,1,0:T(8,128)(2,1)}, bf16[3,1024,12...) while((s32[]{:T(128)}, bf16[3,1024,128]{2,1,0:T(8,128)(2,1)}, ...), condition=%wide.region_7.8_spmd, body=%wide.region_0.7_spmd.sunk | while | flops 979120320 | bytes 70489952 | solution.py:145
  197.4 2.1 gather_fusion.1
  199.5 3.5 fusion.160
  203.8 1.8 fusion.162
  205.6 3.7 convolution_convert_fusion.9
  209.3 8.7 %fusion.163 = bf16[14,64,128]{2,1,0:T(8,128)(2,1)} fusion(bf16[14,512,128]{2,1,0:T(8,128)(2,1)S(1)} %bitcast.148, f32[14,64,512]{2,1,0:T(8,128)} %fusion.160, f32[14,64,512]{2,1,0:T(8,128)} %get-tuple-element.217, f32[14,64]{1,0:T(8,128)S(1)} %get-tuple-element.218), kind=kOutput, calls=%fused_computation.27.clone.1 | convolution fusion | flops 120767872 | bytes 5737984 | tf_op jit(solution)/shard_map/while/body/eval_jaxpr/rqk,rkd->rqd/dot_general | solution.py:31
  218.1 10.8 %fusion.165 = f32[14,512,128]{2,1,0:T(8,128)} fusion(bf16[14,64,128]{2,1,0:T(8,128)(2,1)S(1)} %bitcast.155, f32[14,64,512]{2,1,0:T(8,128)} %fusion.160, f32[14,64,512]{2,1,0:T(8,128)} %get-tuple-element.217, f32[14,64]{1,0:T(8,128)S(1)} %get-tuple-element.218), kind=kOutput, calls=%fused_computation.14.clone.1 | convolution fusion | flops 120653184 | bytes 7572992 | tf_op jit(solution)/shard_map/while/body/eval_jaxpr/rqk,rqd->rkd/dot_general | solution.py:32
  228.9 6.1 %fusion.166 = f32[16,64,128]{2,0,1:T(8,128)S(1)} fusion(f32[14,8,64,128]{3,2,1,0:T(8,128)} %bitcast.151, s32[14,8]{0,1:T(8,128)S(1)} %copy.107), kind=kOutput, calls=%fused_computation.17.clone.1 | convolution fusion | flops 176162560 | bytes 4194752 | tf_op jit(solution)/shard_map/while/body/eval_jaxpr/msn,msbd->nbd/dot_general | solution.py:86
  235.2 2.5 fusion.167
  248.2 2.1 gather_fusion.1
  250.3 3.5 fusion.160
  254.5 1.8 fusion.162
  256.3 3.7 convolution_convert_fusion.9
  260.1 8.7 %fusion.163 = bf16[14,64,128]{2,1,0:T(8,128)(2,1)} fusion(bf16[14,512,128]{2,1,0:T(8,128)(2,1)S(1)} %bitcast.148, f32[14,64,512]{2,1,0:T(8,128)} %fusion.160, f32[14,64,512]{2,1,0:T(8,128)} %get-tuple-element.217, f32[14,64]{1,0:T(8,128)S(1)} %get-tuple-element.218), kind=kOutput, calls=%fused_computation.27.clone.1 | convolution fusion | flops 120767872 | bytes 5737984 | tf_op jit(solution)/shard_map/while/body/eval_jaxpr/rqk,rkd->rqd/dot_general | solution.py:31
  268.8 10.8 %fusion.165 = f32[14,512,128]{2,1,0:T(8,128)} fusion(bf16[14,64,128]{2,1,0:T(8,128)(2,1)S(1)} %bitcast.155, f32[14,64,512]{2,1,0:T(8,128)} %fusion.160, f32[14,64,512]{2,1,0:T(8,128)} %get-tuple-element.217, f32[14,64]{1,0:T(8,128)S(1)} %get-tuple-element.218), kind=kOutput, calls=%fused_computation.14.clone.1 | convolution fusion | flops 120653184 | bytes 7572992 | tf_op jit(solution)/shard_map/while/body/eval_jaxpr/rqk,rqd->rkd/dot_general | solution.py:32
  279.6 6.1 %fusion.166 = f32[16,64,128]{2,0,1:T(8,128)S(1)} fusion(f32[14,8,64,128]{3,2,1,0:T(8,128)} %bitcast.151, s32[14,8]{0,1:T(8,128)S(1)} %copy.107), kind=kOutput, calls=%fused_computation.17.clone.1 | convolution fusion | flops 176162560 | bytes 4194752 | tf_op jit(solution)/shard_map/while/body/eval_jaxpr/msn,msbd->nbd/dot_general | solution.py:86
  285.9 2.4 fusion.167
  298.9 2.1 gather_fusion.1
  301.0 3.5 fusion.160
  305.3 1.8 fusion.162
  307.1 3.7 convolution_convert_fusion.9
  310.8 8.7 %fusion.163 = bf16[14,64,128]{2,1,0:T(8,128)(2,1)} fusion(bf16[14,512,128]{2,1,0:T(8,128)(2,1)S(1)} %bitcast.148, f32[14,64,512]{2,1,0:T(8,128)} %fusion.160, f32[14,64,512]{2,1,0:T(8,128)} %get-tuple-element.217, f32[14,64]{1,0:T(8,128)S(1)} %get-tuple-element.218), kind=kOutput, calls=%fused_computation.27.clone.1 | convolution fusion | flops 120767872 | bytes 5737984 | tf_op jit(solution)/shard_map/while/body/eval_jaxpr/rqk,rkd->rqd/dot_general | solution.py:31
  319.5 10.8 %fusion.165 = f32[14,512,128]{2,1,0:T(8,128)} fusion(bf16[14,64,128]{2,1,0:T(8,128)(2,1)S(1)} %bitcast.155, f32[14,64,512]{2,1,0:T(8,128)} %fusion.160, f32[14,64,512]{2,1,0:T(8,128)} %get-tuple-element.217, f32[14,64]{1,0:T(8,128)S(1)} %get-tuple-element.218), kind=kOutput, calls=%fused_computation.14.clone.1 | convolution fusion | flops 120653184 | bytes 7572992 | tf_op jit(solution)/shard_map/while/body/eval_jaxpr/rqk,rqd->rkd/dot_general | solution.py:32
  330.3 6.1 %fusion.166 = f32[16,64,128]{2,0,1:T(8,128)S(1)} fusion(f32[14,8,64,128]{3,2,1,0:T(8,128)} %bitcast.151, s32[14,8]{0,1:T(8,128)S(1)} %copy.107), kind=kOutput, calls=%fused_computation.17.clone.1 | convolution fusion | flops 176162560 | bytes 4194752 | tf_op jit(solution)/shard_map/while/body/eval_jaxpr/msn,msbd->nbd/dot_general | solution.py:86
  336.6 2.4 fusion.167
  340.4 6.9 %fusion.81 = f32[3,128,2560]{2,1,0:T(8,128)} fusion(bf16[3,1024,128]{2,1,0:T(8,128)(2,1)} %get-tuple-element.59, bf16[1024,2560]{1,0:T(8,128)(2,1)} %all-gather.2.cloned.1.call-done), kind=kOutput, calls=%fused_computation.93 | convolution fusion | flops 2013265920 | bytes 9961472 | tf_op jit(solution)/shard_map/hld,lc->hdc/dot_general | solution.py:109
  347.3 5.5 copy.74
  355.4 5.5 all-to-all-start.5
  362.3 10.7 %all-to-all-done.5 = bf16[8,128,384]{1,2,0:T(8,128)(2,1)S(1)} async-done(((bf16[8,128,384]{1,2,0:T(8,128)(2,1)}), bf16[8,128,384]{1,2,0:T(8,128)(2,1)S(1)}, u32[]{:S(2)}, u32[]{:S(2)}) %all-to-all-start.5) | async-done | bytes 786464 | tf_op jit(solution)/shard_map/all_to_all | solution.py:149
  373.0 4.8 all-to-all-start.4
  377.8 1.2 copy.76
  379.0 9.2 %all-to-all-done.4 = bf16[8,128,384]{1,2,0:T(8,128)(2,1)S(1)} async-done(((bf16[8,128,384]{1,2,0:T(8,128)(2,1)}), bf16[8,128,384]{1,2,0:T(8,128)(2,1)S(1)}, u32[]{:S(2)}, u32[]{:S(2)}) %all-to-all-start.4) | async-done | bytes 786464 | tf_op jit(solution)/shard_map/all_to_all | solution.py:148
  388.1 1.2 copy.75
  389.3 185.9 %reduce-scatter.5.cloned.1.call-done = f32[384,40]{0,1:T(8,128)} async-done(((f32[384,2560]{0,1:T(8,128)}), f32[384,40]{0,1:T(8,128)}) %reduce-scatter.5.cloned.1.call-update) | async-done | bytes 61456
  (202 shorter events, 42.1 us)
Async XLA Ops:
  7.2 79.4 %copy-start = (s32[24,16,16]{0,2,1:T(8,128)S(1)}, s32[24,16,16]{0,2,1:T(8,128)}, u32[]{:S(2)}) copy-start(s32[24,16,16]{0,2,1:T(8,128)} %param.14) | copy-start | bytes 73732
  7.2 12.4 %copy-start.8 = (bf16[128,3072]{1,0:T(8,128)(2,1)S(1)}, bf16[128,3072]{1,0:T(8,128)(2,1)}, u32[]{:S(2)}) copy-start(bf16[128,3072]{1,0:T(8,128)(2,1)} %param.10) | copy-start | bytes 2359300
  9.6 19.1 %all-to-all-start = ((bf16[128,8,384]{0,2,1:T(8,128)(2,1)}), bf16[128,8,384]{0,2,1:T(8,128)(2,1)S(1)}, u32[]{:S(2)}, u32[]{:S(2)}) async-start(bf16[128,8,384]{0,2,1:T(8,128)(2,1)} %bitcast.19), calls=%async_computation | async-start | bytes 1572864 | tf_op jit(solution)/shard_map/all_to_all | solution.py:120
  18.8 15.2 %copy-start.9 = (bf16[128,3072]{1,0:T(8,128)(2,1)S(1)}, bf16[128,3072]{1,0:T(8,128)(2,1)}, u32[]{:S(2)}) copy-start(bf16[128,3072]{1,0:T(8,128)(2,1)} %param.11) | copy-start | bytes 2359300
  18.8 162.8 %all-gather.2.cloned.1.call-start = ((), (), s32[]{:S(2)}) async-start(), calls=%async_computation.7 | async-start | bytes 5898240 | tf_op jit(solution)/shard_map/all_gather | solution.py:124
  28.7 16.5 %all-to-all-start.1 = ((bf16[128,8,384]{0,2,1:T(8,128)(2,1)}), bf16[128,8,384]{0,2,1:T(8,128)(2,1)S(1)}, u32[]{:S(2)}, u32[]{:S(2)}) async-start(bf16[128,8,384]{0,2,1:T(8,128)(2,1)} %bitcast.22), calls=%async_computation.1 | async-start | bytes 1572864 | tf_op jit(solution)/shard_map/all_to_all | solution.py:121
  34.1 31.8 %copy-start.12 = (bf16[384,40]{0,1:T(8,128)(2,1)S(1)}, bf16[384,40]{0,1:T(8,128)(2,1)}, u32[]{:S(2)}) copy-start(bf16[384,40]{0,1:T(8,128)(2,1)} %param.13) | copy-start | bytes 92164
  67.3 19.0 %copy-start.15 = (s32[24,16]{0,1:T(8,128)S(1)}, s32[24,16]{0,1:T(8,128)}, u32[]{:S(2)}) copy-start(s32[24,16]{0,1:T(8,128)} %param.15) | copy-start | bytes 4612
  67.3 114.3 %all-to-all-start.3 = ((bf16[64,384,40]{1,2,0:T(8,128)(2,1)}), bf16[64,384,40]{1,2,0:T(8,128)(2,1)}, u32[]{:S(2)}, u32[]{:S(2)}) async-start(bf16[64,384,40]{1,2,0:T(8,128)(2,1)} %stack.6), calls=%async_computation.3 | async-start | bytes 3932160 | tf_op jit(solution)/shard_map/all_to_all | solution.py:100
  86.3 488.9 %reduce-scatter.5.cloned.1.call-start = ((), (), s32[]{:S(2)}) async-start(), calls=%async_computation.8 | async-start | bytes 3993600
  188.2 2.1 copy-start.16
  188.2 3.6 copy-start.3
  194.4 0.9 copy-start.2
  194.9 1.0 copy-start.13
  203.8 1.8 copy-start.1
  228.8 6.3 %copy-start.14 = (f32[2,64]{1,0:T(2,128)S(1)}, f32[2,64]{1,0:T(2,128)}, u32[]{:S(2)}) copy-start(f32[2,64]{1,0:T(2,128)} %copy-done.13) | copy-start | bytes 1540 | tf_op jit(solution)/shard_map/while
  234.9 2.7 copy-start.5
  235.1 2.5 copy-start.6
  235.1 2.5 copy-start.7
  237.6 1.3 copy-start.4
  237.6 1.3 copy-start.17
  238.9 2.1 copy-start.16
  238.9 3.6 copy-start.3
  245.2 0.9 copy-start.2
  245.6 1.0 copy-start.13
  254.5 1.8 copy-start.1
  279.6 6.3 %copy-start.14 = (f32[2,64]{1,0:T(2,128)S(1)}, f32[2,64]{1,0:T(2,128)}, u32[]{:S(2)}) copy-start(f32[2,64]{1,0:T(2,128)} %copy-done.13) | copy-start | bytes 1540 | tf_op jit(solution)/shard_map/while
  285.7 2.7 copy-start.5
  285.9 2.5 copy-start.6
  285.9 2.5 copy-start.7
  288.4 1.3 copy-start.4
  288.4 1.3 copy-start.17
  289.7 2.1 copy-start.16
  289.7 3.6 copy-start.3
  295.9 0.9 copy-start.2
  296.4 1.0 copy-start.13
  305.3 1.8 copy-start.1
  330.3 6.3 %copy-start.14 = (f32[2,64]{1,0:T(2,128)S(1)}, f32[2,64]{1,0:T(2,128)}, u32[]{:S(2)}) copy-start(f32[2,64]{1,0:T(2,128)} %copy-done.13) | copy-start | bytes 1540 | tf_op jit(solution)/shard_map/while
  336.4 2.7 copy-start.5
  336.6 2.5 copy-start.6
  336.6 2.5 copy-start.7
  339.1 1.3 copy-start.4
  339.1 1.3 copy-start.17
  352.8 1.1 copy-start.10
  354.4 6.5 %copy-start.11 = (bf16[3,1024,128]{2,1,0:T(8,128)(2,1)S(1)}, bf16[3,1024,128]{2,1,0:T(8,128)(2,1)}, u32[]{:S(2)}) copy-start(bf16[3,1024,128]{2,1,0:T(8,128)(2,1)} %get-tuple-element.57) | copy-start | bytes 2359300
  355.4 17.6 %all-to-all-start.5 = ((bf16[8,128,384]{1,2,0:T(8,128)(2,1)}), bf16[8,128,384]{1,2,0:T(8,128)(2,1)S(1)}, u32[]{:S(2)}, u32[]{:S(2)}) async-start(bf16[8,128,384]{1,2,0:T(8,128)(2,1)} %copy.72), calls=%async_computation.5 | async-start | bytes 1572864 | tf_op jit(solution)/shard_map/all_to_all | solution.py:149
  373.0 15.1 %all-to-all-start.4 = ((bf16[8,128,384]{1,2,0:T(8,128)(2,1)}), bf16[8,128,384]{1,2,0:T(8,128)(2,1)S(1)}, u32[]{:S(2)}, u32[]{:S(2)}) async-start(bf16[8,128,384]{1,2,0:T(8,128)(2,1)} %copy.70), calls=%async_computation.4 | async-start | bytes 1572864 | tf_op jit(solution)/shard_map/all_to_all | solution.py:148
Sparse Core Ops, SparseCore 0:
  22.8 113.4 all-gather.1
  352.9 222.2 reduce-scatter.4
